TPU v7x, 32 devices: a whole 2x2x4 slice. The times are simulated.
32 devices in a mesh: phase: 4 (over x, core), seq: 4 (over z), mp: 2 (over y).
Axes of the slice: x: 2, y: 2, z: 4, core: 2. Of those that a mesh axis runs over, the one named last changes fastest.
Arguments:
- queries: bfloat16 [4, 2048, 4096], P('phase', 'seq', 'mp'), may hold values from -360 to 360
- key_weight: bfloat16 [4, 1024, 4096], P('phase', None, 'mp'), may hold values from -0.1875 to 0.1875
- value_weight: bfloat16 [4, 1024, 4096], P('phase', None, 'mp'), may hold values from -0.1875 to 0.1875
- enc_gain: float32 [1024], replicated, may hold values from 0.25 to 2
- neighbour_states: bfloat16 [80, 64, 1024], P('seq', ('phase', 'mp')), may hold values from -600 to 600
- slot_dest: int32 [80], P('seq'), may hold values from -1 to 63, as said below
Outputs:
- context: bfloat16 [4, 2048, 4096], P('phase', 'seq', 'mp')
Inputs may be any that keep to these rules, and one draw needn't show every extreme that they name: slot_dest names every position 0 to 63 exactly once and is -1 elsewhere. Positions 2 * 8 j to 2 * 8 (j + 1) - 1 belong to the tokens of index j of seq. The slots of one index of seq name at most 5 positions of any one index of seq, and this bound is reached; one index of seq has up to 20 filled slots, reached in every draw.
All inputs are finite; a program needn't handle non-finite values.
Results may differ from a plain program's by a relative error of at most 0.0074.
Values may be sent and summed in bfloat16 or wider, within the bound.
No kernel may reach another device: no remote copies, remote signals or barrier semaphores. Data moves between devices by JAX's collectives and lax.ppermute only.
A program may use at most 64 MiB of HBM per device.

v0:
```python
import jax
import jax.numpy as jnp
from jax import lax
from jax.sharding import PartitionSpec as P

HD = 128
SEGLEN = 64
NLEN = 64
NEIGH = 2


def shifted(shard, axis, by):
    peers = lax.axis_size(axis)
    pairs = [(i, i + by) for i in range(peers) if 0 <= i + by < peers]
    return lax.ppermute(shard, axis, pairs)


def normalize(rows, gain):
    states = rows.astype(jnp.float32)
    meansq = jnp.mean(states * states, axis=-1, keepdims=True)
    return (states * lax.rsqrt(meansq + 1e-06) * gain).astype(jnp.bfloat16)


def project(rows, weight):
    flattened = rows.reshape(-1, rows.shape[-1])
    return jnp.dot(flattened, weight, preferred_element_type=jnp.float32).astype(jnp.bfloat16)


def attend(query_win, key_win, value_win):
    windows = query_win.shape[0]
    heads = query_win.shape[2] // HD
    query_four = query_win.reshape(windows, query_win.shape[1], heads, HD)
    key_four = key_win.reshape(windows, key_win.shape[1], heads, HD)
    value_four = value_win.reshape(windows, value_win.shape[1], heads, HD)
    scores = jnp.einsum(
        "wqhd,wkhd->whqk", query_four, key_four, preferred_element_type=jnp.float32
    ) * HD ** (-0.5)
    top = jnp.max(scores, axis=-1, keepdims=True)
    exponent = jnp.exp(scores - top)
    weights = (exponent / jnp.sum(exponent, axis=-1, keepdims=True)).astype(jnp.bfloat16)
    context = jnp.einsum("whqk,wkhd->wqhd", weights, value_four, preferred_element_type=jnp.float32)
    return context.astype(jnp.bfloat16).reshape(windows, query_win.shape[1], heads * HD)


def packing(slot_dest, shards, per_shard, capacity):
    count = slot_dest.shape[0]
    is_live = slot_dest >= 0
    target = jnp.where(is_live, slot_dest // per_shard, -1)
    order = jnp.arange(count)
    earlier = (target[:, None] == target[None, :]) & (order[None, :] < order[:, None])
    slot_rank = jnp.sum(earlier.astype(jnp.int32), axis=1)
    buffer_slot = jnp.where(is_live, target * capacity + slot_rank, -1)
    matches = jnp.arange(shards * capacity)[:, None] == buffer_slot[None, :]
    selector = matches.astype(jnp.bfloat16)
    sent_dest = jnp.sum(jnp.where(matches, slot_dest[None, :] + 1, 0), axis=1) - 1
    return (selector, sent_dest.reshape(shards, capacity))


def pack(selector, rows, shards, capacity):
    flattened = rows.reshape(rows.shape[0], rows.shape[1] * rows.shape[2])
    packed = jnp.dot(selector, flattened, preferred_element_type=jnp.float32).astype(jnp.bfloat16)
    return packed.reshape(shards, capacity, rows.shape[1], rows.shape[2])


def unpack(received, received_dest, own_index, per_shard):
    flat_dest = received_dest.reshape(-1)
    local = jnp.where(flat_dest >= 0, flat_dest - own_index * per_shard, -1)
    placer = (jnp.arange(per_shard)[:, None] == local[None, :]).astype(jnp.bfloat16)
    stacked = received.reshape(flat_dest.shape[0], received.shape[2] * received.shape[3])
    placed = jnp.dot(placer, stacked, preferred_element_type=jnp.float32).astype(jnp.bfloat16)
    return placed.reshape(per_shard, received.shape[2], received.shape[3])


def edge_windows(query_rows, keys, values, prev_keys, prev_values):
    tokens_here = query_rows.shape[0]
    width = query_rows.shape[1]
    blocks = keys.shape[0]
    padded = jnp.concatenate(
        [
            jnp.zeros((1, width), jnp.bfloat16),
            query_rows,
            jnp.zeros((SEGLEN - 1, width), jnp.bfloat16),
        ],
        axis=0,
    )
    padded = padded.reshape(blocks + 1, SEGLEN, width)
    all_keys = jnp.concatenate([prev_keys[None], keys], axis=0)
    all_values = jnp.concatenate([prev_values[None], values], axis=0)
    context = attend(padded, all_keys, all_values)
    return context.reshape((blocks + 1) * SEGLEN, width)[1 : tokens_here + 1]


def on_device(queries, key_weight, value_weight, enc_gain, neighbour_states, slot_dest):
    shards = lax.axis_size("seq")
    own_index = lax.axis_index("seq")
    query_rows = queries[0]
    tokens_here = query_rows.shape[0]
    blocks = tokens_here // SEGLEN
    per_shard = NEIGH * blocks
    capacity = per_shard // shards + 1
    selector, sent_dest = packing(slot_dest, shards, per_shard, capacity)
    received, received_dest = (
        lax.all_to_all(
            pack(selector, neighbour_states, shards, capacity),
            "seq",
            split_axis=0,
            concat_axis=0,
            tiled=True,
        ),
        lax.all_to_all(sent_dest, "seq", split_axis=0, concat_axis=0, tiled=True),
    )
    arranged = unpack(received, received_dest, own_index, per_shard)
    routed = lax.all_gather(arranged, ("phase", "mp"), axis=1, tiled=True)
    neighbours = normalize(routed, enc_gain)
    key_mat = key_weight[0]
    value_mat = value_weight[0]
    width = key_mat.shape[1]
    keys = project(neighbours, key_mat).reshape(blocks, NEIGH * NLEN, width)
    values = project(neighbours, value_mat).reshape(blocks, NEIGH * NLEN, width)
    prev_keys, prev_values = shifted((keys[blocks - 1], values[blocks - 1]), "seq", 1)
    joined = edge_windows(query_rows, keys, values, prev_keys, prev_values)
    position = jnp.arange(tokens_here) + 1
    window_index = own_index * blocks + position // SEGLEN
    silent = (position % SEGLEN != 0) & (window_index == 0)
    result = jnp.where(silent[:, None], jnp.zeros_like(joined), joined)
    return result[None]


def solution(mesh):
    in_specs = (
        P("phase", "seq", "mp"),
        P("phase", None, "mp"),
        P("phase", None, "mp"),
        P(),
        P("seq", ("phase", "mp"), None),
        P("seq"),
    )
    out_specs = P("phase", "seq", "mp")
    return jax.shard_map(
        on_device, mesh=mesh, in_specs=in_specs, out_specs=out_specs, check_vma=False
    )
```

profile of v0, /device:TPU:0, one launch (start us, length us, event | category | flops | bytes accessed | tf_op | source)
XLA Modules:
  0.0 137.3 jit_solution(5685725750526515950)
XLA Ops:
  8.8 6.3 %all-to-all-start = ((s32[4,1,5]{2,1,0:T(1,128)}), s32[4,1,5]{2,1,0:T(1,128)S(1)}, u32[]{:S(2)}, u32[]{:S(2)}) async-start(s32[4,1,5]{2,1,0:T(1,128)} %bitcast), calls=%async_computation | async-start | bytes 4096 | tf_op jit(solution)/shard_map/all_to_all | solution.py:110
  17.7 2.9 %all-to-all-done = s32[4,1,5]{2,1,0:T(1,128)S(1)} async-done(((s32[4,1,5]{2,1,0:T(1,128)}), s32[4,1,5]{2,1,0:T(1,128)S(1)}, u32[]{:S(2)}, u32[]{:S(2)}) %all-to-all-start) | async-done | bytes 112 | tf_op jit(solution)/shard_map/all_to_all | solution.py:110
  20.6 3.5 %all-to-all-start.1 = ((bf16[4,5,8,1024]{3,2,1,0:T(8,128)(2,1)}), bf16[4,5,8,1024]{3,2,1,0:T(8,128)(2,1)S(1)}, u32[]{:S(2)}, u32[]{:S(2)}) async-start(bf16[4,5,8,1024]{3,2,1,0:T(8,128)(2,1)} %bitcast.17), calls=%async_computation.1 | async-start | bytes 655360 | tf_op jit(solution)/shard_map/all_to_all | solution.py:103
  24.2 9.1 %all-to-all-done.1 = bf16[4,5,8,1024]{3,2,1,0:T(8,128)(2,1)S(1)} async-done(((bf16[4,5,8,1024]{3,2,1,0:T(8,128)(2,1)}), bf16[4,5,8,1024]{3,2,1,0:T(8,128)(2,1)S(1)}, u32[]{:S(2)}, u32[]{:S(2)}) %all-to-all-start.1) | async-done | bytes 327712 | tf_op jit(solution)/shard_map/all_to_all | solution.py:103
  34.7 27.0 %all-gather.2.cloned.1.call-done = bf16[16,64,1024]{2,1,0:T(8,128)(2,1)} async-done(((bf16[16,8,1024]{2,1,0:T(8,128)(2,1)}), bf16[16,64,1024]{2,1,0:T(8,128)(2,1)}) %all-gather.2.cloned.1.call-update) | async-done | bytes 2097168 | tf_op jit(solution)/shard_map/all_gather | solution.py:113
  61.7 2.2 %fusion.9 = f32[16,64]{1,0:T(8,128)S(1)} fusion(bf16[16,64,1024]{2,1,0:T(8,128)(2,1)} %all-gather.2.cloned.1.call-done), kind=kLoop, calls=%fused_computation.15 | loop fusion | flops 3144704 | bytes 2101248 | tf_op jit(solution)/shard_map/reduce_sum | solution.py:20
  64.0 2.1 %fusion.11 = bf16[16,64,1024]{2,1,0:T(8,128)(2,1)S(1)} fusion(bf16[16,64,1024]{2,1,0:T(8,128)(2,1)} %all-gather.2.cloned.1.call-done, f32[1024]{0:T(1024)S(1)} %copy-done.6, f32[16,64]{1,0:T(8,128)S(1)} %add_rsqrt_fusion), kind=kLoop, calls=%fused_computation.17 | loop fusion | flops 4194304 | bytes 4202496 | tf_op jit(solution)/shard_map/convert_element_type | solution.py:21
  66.1 4.7 %fusion.20 = bf16[1024,2048]{1,0:T(8,128)(2,1)S(1)} fusion(bf16[1024,1024]{1,0:T(8,128)(2,1)S(1)} %bitcast.64, bf16[1,1024,2048]{2,1,0:T(8,128)(2,1)S(1)} %copy-done.7), kind=kOutput, calls=%fused_computation.25 | convolution fusion | flops 4297064448 | bytes 10485760 | tf_op jit(solution)/shard_map/dot_general | solution.py:26
  71.8 3.7 %collective-permute-start.1 = (bf16[128,2048]{1,0:T(8,128)(2,1)}, bf16[128,2048]{1,0:T(8,128)(2,1)S(1)}, u32[]{:S(2)}, u32[]{:S(2)}) collective-permute-start(bf16[128,2048]{1,0:T(8,128)(2,1)} %slice.14), channel_id=1, source_target_pairs={{0,2},{2,4},{4,6},{1,3},{3,5},{5,7},{8,10},{10,12},{12,14},{9,11},... | collective-permute-start | bytes 1572872 | tf_op jit(solution)/shard_map/ppermute | solution.py:15
  75.4 4.7 %fusion.17 = bf16[1024,2048]{1,0:T(8,128)(2,1)S(1)} fusion(bf16[1024,1024]{1,0:T(8,128)(2,1)S(1)} %bitcast.65, bf16[1,1024,2048]{2,1,0:T(8,128)(2,1)S(1)} %copy-done.8), kind=kOutput, calls=%fused_computation.24 | convolution fusion | flops 4297064448 | bytes 10485760 | tf_op jit(solution)/shard_map/dot_general | solution.py:26
  81.1 1.3 copy-done.2
  82.4 3.6 %collective-permute-start = (bf16[128,2048]{1,0:T(8,128)(2,1)}, bf16[128,2048]{1,0:T(8,128)(2,1)S(1)}, u32[]{:S(2)}, u32[]{:S(2)}) collective-permute-start(bf16[128,2048]{1,0:T(8,128)(2,1)} %slice.15), channel_id=1, source_target_pairs={{0,2},{2,4},{4,6},{1,3},{3,5},{5,7},{8,10},{10,12},{12,14},{9,11},... | collective-permute-start | bytes 1572872 | tf_op jit(solution)/shard_map/ppermute | solution.py:15
  86.0 1.0 maximum_bitcast_fusion
  88.2 1.4 %copy.39 = bf16[128,8,16,128]{3,2,1,0:T(8,128)(2,1)S(1)} copy(bf16[128,8,16,128]{3,1,2,0:T(8,128)(2,1)S(1)} %bitcast.62) | data formatting | bytes 8388608
  89.7 3.2 %copy.26 = bf16[8,128,16,128]{3,1,2,0:T(8,128)(2,1)} copy(bf16[8,128,16,128]{3,2,1,0:T(8,128)(2,1)S(1)} %bitcast.56) | data formatting | bytes 8388608 | tf_op jit(solution)/shard_map/concatenate | solution.py:88
  92.8 1.4 %copy.37 = bf16[128,8,16,128]{3,2,1,0:T(8,128)(2,1)S(1)} copy(bf16[128,8,16,128]{3,1,2,0:T(8,128)(2,1)S(1)} %bitcast.61) | data formatting | bytes 8388608
  94.3 1.2 copy.28
  95.7 2.8 %collective-permute-done = bf16[128,2048]{1,0:T(8,128)(2,1)S(1)} collective-permute-done((bf16[128,2048]{1,0:T(8,128)(2,1)}, bf16[128,2048]{1,0:T(8,128)(2,1)S(1)}, u32[]{:S(2)}, u32[]{:S(2)}) %collective-permute-start) | collective-permute-done | bytes 524320 | tf_op jit(solution)/shard_map/ppermute | solution.py:15
  98.8 3.3 %fusion.1 = f32[9,16,64,128]{3,2,1,0:T(8,128)S(1)} fusion(bf16[8,128,16,128]{3,1,2,0:T(8,128)(2,1)S(1)} %copy.28, bf16[1,128,16,128]{3,1,2,0:T(8,128)(2,1)S(1)} %copy.27, bf16[9,64,16,128]{3,2,1,0:T(8,128)(2,1)S(1)} %bitcast.59), kind=kOutput, calls=%fused_computation.5 | convolution fusion | flops 304349184 | bytes 11796480 | tf_op jit(solution)/shard_map/wqhd,wkhd->whqk/dot_general | solution.py:35
  102.1 2.1 %copy-done.4 = f32[9,16,64,128]{3,2,1,0:T(8,128)} copy-done((f32[9,16,64,128]{3,2,1,0:T(8,128)}, f32[9,16,64,128]{3,2,1,0:T(8,128)S(1)}, u32[]{:S(2)}) %copy-start.4) | copy-done | bytes 4718616
  104.2 2.5 %fusion.51 = f32[9,16,64]{2,1,0:T(8,128)S(1)} fusion(f32[9,16,64,128]{3,2,1,0:T(8,128)S(1)} %fusion.1), kind=kOutput, calls=%fused_computation.71 | output fusion | flops 4718719 | bytes 4755456 | tf_op jit(solution)/shard_map/sub | solution.py:39
  106.7 19.5 %convert_bitcast_fusion = bf16[9,64,16,128]{3,1,2,0:T(8,128)(2,1)S(1)} fusion(bf16[8,128,16,128]{3,1,2,0:T(8,128)(2,1)} %copy.26, bf16[1,128,16,128]{3,1,2,0:T(8,128)(2,1)S(1)} %copy.25, f32[9,16,64]{2,1,0:T(8,128)S(1)} %fusion.51, f32[9,16,64,128]{3,2,1,0:T(8,128)} %copy-done.4), kind=kOutput, calls=%fused_computation.29 | convolution fusion | flops 318514304 | bytes 11833344 | tf_op jit(solution)/shard_map/whqk,wkhd->wqhd/dot_general | solution.py:41
  126.2 1.6 %copy.30 = bf16[9,64,16,128]{3,2,1,0:T(8,128)(2,1)S(1)} copy(bf16[9,64,16,128]{3,1,2,0:T(8,128)(2,1)S(1)} %convert_bitcast_fusion) | data formatting | bytes 4718592 | tf_op jit(solution)/shard_map/convert_element_type | solution.py:42
  128.5 2.0 %fusion.28 = bf16[1,512,2048]{2,1,0:T(8,128)(2,1)} fusion(bf16[576,2048]{1,0:T(8,128)(2,1)S(1)} %bitcast.60, pred[512]{0:T(512)(128)(4,1)S(1)} %fusion.44), kind=kLoop, calls=%fused_computation.33 | loop fusion | flops 1048576 | bytes 4194816 | tf_op jit(solution)/shard_map/broadcast_in_dim | solution.py:126
  (49 shorter events, 10.4 us)
Async XLA Ops:
  8.8 11.8 %all-to-all-start = ((s32[4,1,5]{2,1,0:T(1,128)}), s32[4,1,5]{2,1,0:T(1,128)S(1)}, u32[]{:S(2)}, u32[]{:S(2)}) async-start(s32[4,1,5]{2,1,0:T(1,128)} %bitcast), calls=%async_computation | async-start | bytes 4096 | tf_op jit(solution)/shard_map/all_to_all | solution.py:110
  16.2 47.8 %copy-start.6 = (f32[1024]{0:T(1024)S(1)}, f32[1024]{0:T(1024)}, u32[]{:S(2)}) copy-start(f32[1024]{0:T(1024)} %param.9) | copy-start | bytes 12292
  20.6 12.7 %all-to-all-start.1 = ((bf16[4,5,8,1024]{3,2,1,0:T(8,128)(2,1)}), bf16[4,5,8,1024]{3,2,1,0:T(8,128)(2,1)S(1)}, u32[]{:S(2)}, u32[]{:S(2)}) async-start(bf16[4,5,8,1024]{3,2,1,0:T(8,128)(2,1)} %bitcast.17), calls=%async_computation.1 | async-start | bytes 655360 | tf_op jit(solution)/shard_map/all_to_all | solution.py:103
  24.1 37.6 %all-gather.2.cloned.1.call-start = ((), (), s32[]{:S(2)}) async-start(), calls=%async_computation.2 | async-start | bytes 2359296 | tf_op jit(solution)/shard_map/all_gather | solution.py:113
  61.7 4.4 %copy-start.7 = (bf16[1,1024,2048]{2,1,0:T(8,128)(2,1)S(1)}, bf16[1,1024,2048]{2,1,0:T(8,128)(2,1)}, u32[]{:S(2)}) copy-start(bf16[1,1024,2048]{2,1,0:T(8,128)(2,1)} %param.7) | copy-start | bytes 12582916
  66.1 9.3 %copy-start.8 = (bf16[1,1024,2048]{2,1,0:T(8,128)(2,1)S(1)}, bf16[1,1024,2048]{2,1,0:T(8,128)(2,1)}, u32[]{:S(2)}) copy-start(bf16[1,1024,2048]{2,1,0:T(8,128)(2,1)} %param.8) | copy-start | bytes 12582916
  70.9 9.3 %copy-start = (bf16[1024,2048]{1,0:T(8,128)(2,1)}, bf16[1024,2048]{1,0:T(8,128)(2,1)S(1)}, u32[]{:S(2)}) copy-start(bf16[1024,2048]{1,0:T(8,128)(2,1)S(1)} %fusion.20) | copy-start | bytes 12582916
  71.8 14.3 %copy-start.5 = (bf16[1,512,2048]{2,1,0:T(8,128)(2,1)S(1)}, bf16[1,512,2048]{2,1,0:T(8,128)(2,1)}, u32[]{:S(2)}) copy-start(bf16[1,512,2048]{2,1,0:T(8,128)(2,1)} %param.6) | copy-start | bytes 6291460
  71.8 23.7 %collective-permute-start.1 = (bf16[128,2048]{1,0:T(8,128)(2,1)}, bf16[128,2048]{1,0:T(8,128)(2,1)S(1)}, u32[]{:S(2)}, u32[]{:S(2)}) collective-permute-start(bf16[128,2048]{1,0:T(8,128)(2,1)} %slice.14), channel_id=1, source_target_pairs={{0,2},{2,4},{4,6},{1,3},{3,5},{5,7},{8,10},{10,12},{12,14},{9,11},... | collective-permute-start | bytes 1572872 | tf_op jit(solution)/shard_map/ppermute | solution.py:15
  80.2 2.2 %copy-start.2 = (bf16[1024,2048]{1,0:T(8,128)(2,1)}, bf16[1024,2048]{1,0:T(8,128)(2,1)S(1)}, u32[]{:S(2)}) copy-start(bf16[1024,2048]{1,0:T(8,128)(2,1)S(1)} %fusion.17) | copy-start | bytes 12582916
  82.4 16.1 %collective-permute-start = (bf16[128,2048]{1,0:T(8,128)(2,1)}, bf16[128,2048]{1,0:T(8,128)(2,1)S(1)}, u32[]{:S(2)}, u32[]{:S(2)}) collective-permute-start(bf16[128,2048]{1,0:T(8,128)(2,1)} %slice.15), channel_id=1, source_target_pairs={{0,2},{2,4},{4,6},{1,3},{3,5},{5,7},{8,10},{10,12},{12,14},{9,11},... | collective-permute-start | bytes 1572872 | tf_op jit(solution)/shard_map/ppermute | solution.py:15
  86.0 2.2 %copy-start.3 = (bf16[1024,2048]{1,0:T(8,128)(2,1)S(1)}, bf16[1024,2048]{1,0:T(8,128)(2,1)}, u32[]{:S(2)}) copy-start(bf16[1024,2048]{1,0:T(8,128)(2,1)} %copy-done.2) | copy-start | bytes 12582916
  89.6 3.2 %copy-start.1 = (bf16[1024,2048]{1,0:T(8,128)(2,1)S(1)}, bf16[1024,2048]{1,0:T(8,128)(2,1)}, u32[]{:S(2)}) copy-start(bf16[1024,2048]{1,0:T(8,128)(2,1)} %copy-done) | copy-start | bytes 12582916
  102.1 2.1 %copy-start.4 = (f32[9,16,64,128]{3,2,1,0:T(8,128)}, f32[9,16,64,128]{3,2,1,0:T(8,128)S(1)}, u32[]{:S(2)}) copy-start(f32[9,16,64,128]{3,2,1,0:T(8,128)S(1)} %fusion.1) | copy-start | bytes 14155780
Sparse Core Ops, SparseCore 0:
  34.8 26.8 all-gather.1
where the time goes:
time: 138 us; the launch traced here: 137 us
  waiting for transfers between devices  41.9 us (30%)
  matrix products  32.7 us (24%)
  local copies, waits for them, and re-layouts  20.4 us (15%)
  starting transfers between devices  17.1 us (12%)
  between operations  13.7 us (10%)
  other arithmetic  11.6 us (8%)
    all_gather x1, waiting for transfers between devices, on_device(): routed = lax.all_gather(arranged, ('phase', 'mp'), axis=1, tiled=True)  27 us
    dot_general x1, matrix products, attend(): jnp.einsum('whqk,wkhd->wqhd', weights, value_four, preferred_element_type...  19.5 us
    unnamed x31, local copies, waits for them, and re-layouts  11.5 us
    dot_general x2, matrix products, project(): jnp.dot(flattened, weight, preferred_element_type=jnp.float32)  9.46 us
    all_to_all x1, waiting for transfers between devices, on_device(): lax.all_to_all(pack(selector, neighbour_states, shards, capacity), 'seq',...  9.08 us
    ppermute x2, starting transfers between devices, shifted(): return lax.ppermute(shard, axis, pairs)  7.23 us
    all_to_all x1, starting transfers between devices, on_device(): lax.all_to_all(sent_dest, 'seq', split_axis=0, concat_axis=0, tiled=True)  6.35 us
    all_to_all x1, starting transfers between devices, on_device(): lax.all_to_all(pack(selector, neighbour_states, shards, capacity), 'seq',...  3.45 us
  transfers between devices with their start and end apart: 5, of which 4 were waited for; matrix products, arithmetic and copies ran while one was open for 13% of the time, Pallas kernels for 0%

commit v1 on v0

--- a/solution.py
+++ b/solution.py
@@ -110,7 +110,18 @@
         lax.all_to_all(sent_dest, "seq", split_axis=0, concat_axis=0, tiled=True),
     )
     arranged = unpack(received, received_dest, own_index, per_shard)
-    routed = lax.all_gather(arranged, ("phase", "mp"), axis=1, tiled=True)
+    raw_out = jax.lax.axis_size(("phase", "mp"))
+    p_next = jax.lax.axis_index(("phase", "mp"))
+    row_out, y1 = (raw_out, p_next)
+    routed, x_now = (arranged, 1)
+    while x_now < row_out:
+        newest = jax.lax.ppermute(
+            routed, ("phase", "mp"), perm=[(dd, dd ^ x_now) for dd in range(row_out)]
+        )
+        current_value = jnp.concatenate([routed, newest], 1)
+        high = jnp.concatenate([newest, routed], 1)
+        routed = jnp.where(y1 & x_now == 0, current_value, high)
+        x_now = 2 * x_now
     neighbours = normalize(routed, enc_gain)
     key_mat = key_weight[0]
     value_mat = value_weight[0]

time: 138 us -> 126 us (0.913)
  between operations: 13.7 us -> 0.34 us
  waiting for transfers between devices: 41.9 us -> 45.6 us
  other arithmetic: 11.6 us -> 9.35 us
    ppermute x0 -> x3, waiting for transfers between devices: none -> 30.4 us  [on_device(): jax.lax.ppermute(routed, ('phase', 'mp'), perm=[(dd, dd ^ x_now) for dd i...]
    all_gather x1 -> x0, waiting for transfers between devices: 27 us -> none  [on_device(): routed = lax.all_gather(arranged, ('phase', 'mp'), axis=1, tiled=True)]
    ppermute x0 -> x3, starting transfers between devices: none -> 3.22 us  [on_device(): jax.lax.ppermute(routed, ('phase', 'mp'), perm=[(dd, dd ^ x_now) for dd i...]
    ppermute x2, starting transfers between devices: 7.23 us -> 4.51 us  [shifted(): return lax.ppermute(shard, axis, pairs)]
    reduce_sum x1, other arithmetic: 2.22 us -> 0.72 us  [normalize(): meansq = jnp.mean(states * states, axis=-1, keepdims=True)]
  transfers between devices with their start and end apart: 5 -> 7, of which waited for: 4 -> 6; matrix products, arithmetic and copies ran while one was open for 13% -> 14% of each run, Pallas kernels for 0% -> 0%
where the time goes in v1:
time: 126 us; the launch traced here: 125 us
  waiting for transfers between devices  45.6 us (36%)
  matrix products  32.7 us (26%)
  local copies, waits for them, and re-layouts  19.7 us (16%)
  starting transfers between devices  17.7 us (14%)
  other arithmetic  9.35 us (7%)
    ppermute x3, waiting for transfers between devices, on_device(): jax.lax.ppermute(routed, ('phase', 'mp'), perm=[(dd, dd ^ x_now) for dd i...  30.4 us
    dot_general x1, matrix products, attend(): jnp.einsum('whqk,wkhd->wqhd', weights, value_four, preferred_element_type...  19.5 us
    unnamed x31, local copies, waits for them, and re-layouts  10.8 us
    dot_general x2, matrix products, project(): jnp.dot(flattened, weight, preferred_element_type=jnp.float32)  9.46 us
    all_to_all x1, waiting for transfers between devices, on_device(): lax.all_to_all(pack(selector, neighbour_states, shards, capacity), 'seq',...  9.13 us
    all_to_all x1, starting transfers between devices, on_device(): lax.all_to_all(sent_dest, 'seq', split_axis=0, concat_axis=0, tiled=True)  6.35 us
    ppermute x2, starting transfers between devices, shifted(): return lax.ppermute(shard, axis, pairs)  4.51 us
    all_to_all x1, starting transfers between devices, on_device(): lax.all_to_all(pack(selector, neighbour_states, shards, capacity), 'seq',...  3.59 us
  transfers between devices with their start and end apart: 7, of which 6 were waited for; matrix products, arithmetic and copies ran while one was open for 14% of the time, Pallas kernels for 0%

profile of v1, /device:TPU:0, one launch (start us, length us, event | category | flops | bytes accessed | tf_op | source)
XLA Modules:
  0.0 125.3 jit_solution(7274025570280008256)
XLA Ops:
  2.3 6.3 %all-to-all-start = ((s32[4,1,5]{2,1,0:T(1,128)}), s32[4,1,5]{2,1,0:T(1,128)S(1)}, u32[]{:S(2)}, u32[]{:S(2)}) async-start(s32[4,1,5]{2,1,0:T(1,128)} %bitcast), calls=%async_computation | async-start | bytes 4096 | tf_op jit(solution)/shard_map/all_to_all | solution.py:110
  11.1 2.9 %all-to-all-done = s32[4,1,5]{2,1,0:T(1,128)S(1)} async-done(((s32[4,1,5]{2,1,0:T(1,128)}), s32[4,1,5]{2,1,0:T(1,128)S(1)}, u32[]{:S(2)}, u32[]{:S(2)}) %all-to-all-start) | async-done | bytes 112 | tf_op jit(solution)/shard_map/all_to_all | solution.py:110
  14.1 3.6 %all-to-all-start.1 = ((bf16[4,5,8,1024]{3,2,1,0:T(8,128)(2,1)}), bf16[4,5,8,1024]{3,2,1,0:T(8,128)(2,1)S(1)}, u32[]{:S(2)}, u32[]{:S(2)}) async-start(bf16[4,5,8,1024]{3,2,1,0:T(8,128)(2,1)} %bitcast.17), calls=%async_computation.1 | async-start | bytes 655360 | tf_op jit(solution)/shard_map/all_to_all | solution.py:103
  17.8 9.1 %all-to-all-done.1 = bf16[4,5,8,1024]{3,2,1,0:T(8,128)(2,1)S(1)} async-done(((bf16[4,5,8,1024]{3,2,1,0:T(8,128)(2,1)}), bf16[4,5,8,1024]{3,2,1,0:T(8,128)(2,1)S(1)}, u32[]{:S(2)}, u32[]{:S(2)}) %all-to-all-start.1) | async-done | bytes 327712 | tf_op jit(solution)/shard_map/all_to_all | solution.py:103
  27.6 1.6 %collective-permute-start = (bf16[16,8,1024]{2,1,0:T(8,128)(2,1)S(1)}, bf16[16,8,1024]{2,1,0:T(8,128)(2,1)S(1)}, u32[]{:S(2)}, u32[]{:S(2)}) collective-permute-start(bf16[16,8,1024]{2,1,0:T(8,128)(2,1)S(1)} %bitcast.76), channel_id=1, source_target_pairs={{0,1},{1,0},{8,9},{9,8},{16,17},{17,16},{24,25},{25,24},{2,3},{3,2... | collective-permute-start | bytes 786440 | tf_op jit(solution)/shard_map/ppermute | solution.py:118
  29.2 4.8 %collective-permute-done = bf16[16,8,1024]{2,1,0:T(8,128)(2,1)S(1)} collective-permute-done((bf16[16,8,1024]{2,1,0:T(8,128)(2,1)S(1)}, bf16[16,8,1024]{2,1,0:T(8,128)(2,1)S(1)}, u32[]{:S(2)}, u32[]{:S(2)}) %collective-permute-start) | collective-permute-done | bytes 262176 | tf_op jit(solution)/shard_map/ppermute | solution.py:118
  34.2 1.9 %collective-permute-done.1 = bf16[16,16,1024]{2,1,0:T(8,128)(2,1)S(1)} collective-permute-done((bf16[16,16,1024]{2,1,0:T(8,128)(2,1)S(1)}, bf16[16,16,1024]{2,1,0:T(8,128)(2,1)S(1)}, u32[]{:S(2)}, u32[]{:S(2)}) %collective-permute-start.1) | collective-permute-done | bytes 524320 | tf_op jit(solution)/shard_map/ppermute | solution.py:118
  36.6 1.6 %collective-permute-start.2 = (bf16[16,32,1024]{2,1,0:T(8,128)(2,1)S(1)}, bf16[16,32,1024]{2,1,0:T(8,128)(2,1)S(1)}, u32[]{:S(2)}, u32[]{:S(2)}) collective-permute-start(bf16[16,32,1024]{2,1,0:T(8,128)(2,1)S(1)} %maximum_select_fusion.1), channel_id=1, source_target_pairs={{0,16},{1,17},{8,24},{9,25},{16,0},{17,1},{24,8},{25,9},{2,18},{3,... | collective-permute-start | bytes 3145736 | tf_op jit(solution)/shard_map/ppermute | solution.py:118
  38.2 23.7 %collective-permute-done.2 = bf16[16,32,1024]{2,1,0:T(8,128)(2,1)S(1)} collective-permute-done((bf16[16,32,1024]{2,1,0:T(8,128)(2,1)S(1)}, bf16[16,32,1024]{2,1,0:T(8,128)(2,1)S(1)}, u32[]{:S(2)}, u32[]{:S(2)}) %collective-permute-start.2) | collective-permute-done | bytes 1048608 | tf_op jit(solution)/shard_map/ppermute | solution.py:118
  63.4 4.7 %fusion.20 = bf16[1024,2048]{1,0:T(8,128)(2,1)S(1)} fusion(bf16[1024,1024]{1,0:T(8,128)(2,1)S(1)} %bitcast.64, bf16[1,1024,2048]{2,1,0:T(8,128)(2,1)S(1)} %copy-done.7), kind=kOutput, calls=%fused_computation.25 | convolution fusion | flops 4297064448 | bytes 10485760 | tf_op jit(solution)/shard_map/dot_general | solution.py:26
  69.1 2.0 %collective-permute-start.4 = (bf16[128,2048]{1,0:T(8,128)(2,1)}, bf16[128,2048]{1,0:T(8,128)(2,1)S(1)}, u32[]{:S(2)}, u32[]{:S(2)}) collective-permute-start(bf16[128,2048]{1,0:T(8,128)(2,1)} %slice.14), channel_id=1, source_target_pairs={{0,2},{2,4},{4,6},{1,3},{3,5},{5,7},{8,10},{10,12},{12,14},{9,11},... | collective-permute-start | bytes 1572872 | tf_op jit(solution)/shard_map/ppermute | solution.py:15
  71.1 4.7 %fusion.17 = bf16[1024,2048]{1,0:T(8,128)(2,1)S(1)} fusion(bf16[1024,1024]{1,0:T(8,128)(2,1)S(1)} %bitcast.65, bf16[1,1024,2048]{2,1,0:T(8,128)(2,1)S(1)} %copy-done.8), kind=kOutput, calls=%fused_computation.24 | convolution fusion | flops 4297064448 | bytes 10485760 | tf_op jit(solution)/shard_map/dot_general | solution.py:26
  76.8 1.3 %copy-done.2 = bf16[1024,2048]{1,0:T(8,128)(2,1)} copy-done((bf16[1024,2048]{1,0:T(8,128)(2,1)}, bf16[1024,2048]{1,0:T(8,128)(2,1)S(1)}, u32[]{:S(2)}) %copy-start.2) | copy-done | bytes 4194328
  78.1 2.5 %collective-permute-start.3 = (bf16[128,2048]{1,0:T(8,128)(2,1)}, bf16[128,2048]{1,0:T(8,128)(2,1)S(1)}, u32[]{:S(2)}, u32[]{:S(2)}) collective-permute-start(bf16[128,2048]{1,0:T(8,128)(2,1)} %slice.15), channel_id=1, source_target_pairs={{0,2},{2,4},{4,6},{1,3},{3,5},{5,7},{8,10},{10,12},{12,14},{9,11},... | collective-permute-start | bytes 1572872 | tf_op jit(solution)/shard_map/ppermute | solution.py:15
  82.8 1.4 %copy.39 = bf16[128,8,16,128]{3,2,1,0:T(8,128)(2,1)S(1)} copy(bf16[128,8,16,128]{3,1,2,0:T(8,128)(2,1)S(1)} %bitcast.62) | data formatting | bytes 8388608
  84.2 3.2 %copy.26 = bf16[8,128,16,128]{3,1,2,0:T(8,128)(2,1)} copy(bf16[8,128,16,128]{3,2,1,0:T(8,128)(2,1)S(1)} %bitcast.56) | data formatting | bytes 8388608 | tf_op jit(solution)/shard_map/concatenate | solution.py:88
  87.4 1.4 %copy.37 = bf16[128,8,16,128]{3,2,1,0:T(8,128)(2,1)S(1)} copy(bf16[128,8,16,128]{3,1,2,0:T(8,128)(2,1)S(1)} %bitcast.61) | data formatting | bytes 8388608
  90.3 3.1 %collective-permute-done.3 = bf16[128,2048]{1,0:T(8,128)(2,1)S(1)} collective-permute-done((bf16[128,2048]{1,0:T(8,128)(2,1)}, bf16[128,2048]{1,0:T(8,128)(2,1)S(1)}, u32[]{:S(2)}, u32[]{:S(2)}) %collective-permute-start.3) | collective-permute-done | bytes 524320 | tf_op jit(solution)/shard_map/ppermute | solution.py:15
  93.6 3.3 %fusion.1 = f32[9,16,64,128]{3,2,1,0:T(8,128)S(1)} fusion(bf16[8,128,16,128]{3,1,2,0:T(8,128)(2,1)S(1)} %copy.28, bf16[1,128,16,128]{3,1,2,0:T(8,128)(2,1)S(1)} %copy.27, bf16[9,64,16,128]{3,2,1,0:T(8,128)(2,1)S(1)} %bitcast.59), kind=kOutput, calls=%fused_computation.5 | convolution fusion | flops 304349184 | bytes 11796480 | tf_op jit(solution)/shard_map/wqhd,wkhd->whqk/dot_general | solution.py:35
  97.0 2.1 %copy-done.4 = f32[9,16,64,128]{3,2,1,0:T(8,128)} copy-done((f32[9,16,64,128]{3,2,1,0:T(8,128)}, f32[9,16,64,128]{3,2,1,0:T(8,128)S(1)}, u32[]{:S(2)}) %copy-start.4) | copy-done | bytes 4718616
  99.1 2.5 %fusion.51 = f32[9,16,64]{2,1,0:T(8,128)S(1)} fusion(f32[9,16,64,128]{3,2,1,0:T(8,128)S(1)} %fusion.1), kind=kOutput, calls=%fused_computation.74 | output fusion | flops 4718719 | bytes 4755456 | tf_op jit(solution)/shard_map/sub | solution.py:39
  101.6 19.5 %convert_bitcast_fusion = bf16[9,64,16,128]{3,1,2,0:T(8,128)(2,1)S(1)} fusion(bf16[8,128,16,128]{3,1,2,0:T(8,128)(2,1)} %copy.26, bf16[1,128,16,128]{3,1,2,0:T(8,128)(2,1)S(1)} %copy.25, f32[9,16,64]{2,1,0:T(8,128)S(1)} %fusion.51, f32[9,16,64,128]{3,2,1,0:T(8,128)} %copy-done.4), kind=kOutput, calls=%fused_computation.29 | convolution fusion | flops 318514304 | bytes 11833344 | tf_op jit(solution)/shard_map/whqk,wkhd->wqhd/dot_general | solution.py:41
  121.1 1.6 %copy.30 = bf16[9,64,16,128]{3,2,1,0:T(8,128)(2,1)S(1)} copy(bf16[9,64,16,128]{3,1,2,0:T(8,128)(2,1)S(1)} %convert_bitcast_fusion) | data formatting | bytes 4718592 | tf_op jit(solution)/shard_map/convert_element_type | solution.py:42
  123.3 2.0 %fusion.28 = bf16[1,512,2048]{2,1,0:T(8,128)(2,1)} fusion(bf16[576,2048]{1,0:T(8,128)(2,1)S(1)} %bitcast.60, pred[512]{0:T(512)(128)(4,1)S(1)} %fusion.44), kind=kLoop, calls=%fused_computation.33 | loop fusion | flops 1048576 | bytes 4194816 | tf_op jit(solution)/shard_map/broadcast_in_dim | solution.py:137
  (54 shorter events, 14.1 us)
Async XLA Ops:
  2.3 11.8 %all-to-all-start = ((s32[4,1,5]{2,1,0:T(1,128)}), s32[4,1,5]{2,1,0:T(1,128)S(1)}, u32[]{:S(2)}, u32[]{:S(2)}) async-start(s32[4,1,5]{2,1,0:T(1,128)} %bitcast), calls=%async_computation | async-start | bytes 4096 | tf_op jit(solution)/shard_map/all_to_all | solution.py:110
  14.1 48.5 %copy-start.6 = (f32[1024]{0:T(1024)S(1)}, f32[1024]{0:T(1024)}, u32[]{:S(2)}) copy-start(f32[1024]{0:T(1024)} %param.9) | copy-start | bytes 12292
  14.1 12.8 %all-to-all-start.1 = ((bf16[4,5,8,1024]{3,2,1,0:T(8,128)(2,1)}), bf16[4,5,8,1024]{3,2,1,0:T(8,128)(2,1)S(1)}, u32[]{:S(2)}, u32[]{:S(2)}) async-start(bf16[4,5,8,1024]{3,2,1,0:T(8,128)(2,1)} %bitcast.17), calls=%async_computation.1 | async-start | bytes 655360 | tf_op jit(solution)/shard_map/all_to_all | solution.py:103
  27.6 6.4 %collective-permute-start = (bf16[16,8,1024]{2,1,0:T(8,128)(2,1)S(1)}, bf16[16,8,1024]{2,1,0:T(8,128)(2,1)S(1)}, u32[]{:S(2)}, u32[]{:S(2)}) collective-permute-start(bf16[16,8,1024]{2,1,0:T(8,128)(2,1)S(1)} %bitcast.76), channel_id=1, source_target_pairs={{0,1},{1,0},{8,9},{9,8},{16,17},{17,16},{24,25},{25,24},{2,3},{3,2... | collective-permute-start | bytes 786440 | tf_op jit(solution)/shard_map/ppermute | solution.py:118
  34.1 2.0 %collective-permute-start.1 = (bf16[16,16,1024]{2,1,0:T(8,128)(2,1)S(1)}, bf16[16,16,1024]{2,1,0:T(8,128)(2,1)S(1)}, u32[]{:S(2)}, u32[]{:S(2)}) collective-permute-start(bf16[16,16,1024]{2,1,0:T(8,128)(2,1)S(1)} %maximum_select_fusion.2), channel_id=1, source_target_pairs={{0,8},{1,9},{8,0},{9,1},{16,24},{17,25},{24,16},{25,17},{2,10},{3,... | collective-permute-start | bytes 1572872 | tf_op jit(solution)/shard_map/ppermute | solution.py:118
  36.6 25.3 %collective-permute-start.2 = (bf16[16,32,1024]{2,1,0:T(8,128)(2,1)S(1)}, bf16[16,32,1024]{2,1,0:T(8,128)(2,1)S(1)}, u32[]{:S(2)}, u32[]{:S(2)}) collective-permute-start(bf16[16,32,1024]{2,1,0:T(8,128)(2,1)S(1)} %maximum_select_fusion.1), channel_id=1, source_target_pairs={{0,16},{1,17},{8,24},{9,25},{16,0},{17,1},{24,8},{25,9},{2,18},{3,... | collective-permute-start | bytes 3145736 | tf_op jit(solution)/shard_map/ppermute | solution.py:118
  38.2 25.3 %copy-start.7 = (bf16[1,1024,2048]{2,1,0:T(8,128)(2,1)S(1)}, bf16[1,1024,2048]{2,1,0:T(8,128)(2,1)}, u32[]{:S(2)}) copy-start(bf16[1,1024,2048]{2,1,0:T(8,128)(2,1)} %param.7) | copy-start | bytes 12582916
  63.4 7.7 %copy-start.8 = (bf16[1,1024,2048]{2,1,0:T(8,128)(2,1)S(1)}, bf16[1,1024,2048]{2,1,0:T(8,128)(2,1)}, u32[]{:S(2)}) copy-start(bf16[1,1024,2048]{2,1,0:T(8,128)(2,1)} %param.8) | copy-start | bytes 12582916
  68.2 7.7 %copy-start = (bf16[1024,2048]{1,0:T(8,128)(2,1)}, bf16[1024,2048]{1,0:T(8,128)(2,1)S(1)}, u32[]{:S(2)}) copy-start(bf16[1024,2048]{1,0:T(8,128)(2,1)S(1)} %fusion.20) | copy-start | bytes 12582916
  69.1 11.6 %copy-start.5 = (bf16[1,512,2048]{2,1,0:T(8,128)(2,1)S(1)}, bf16[1,512,2048]{2,1,0:T(8,128)(2,1)}, u32[]{:S(2)}) copy-start(bf16[1,512,2048]{2,1,0:T(8,128)(2,1)} %param.6) | copy-start | bytes 6291460
  69.1 21.0 %collective-permute-start.4 = (bf16[128,2048]{1,0:T(8,128)(2,1)}, bf16[128,2048]{1,0:T(8,128)(2,1)S(1)}, u32[]{:S(2)}, u32[]{:S(2)}) collective-permute-start(bf16[128,2048]{1,0:T(8,128)(2,1)} %slice.14), channel_id=1, source_target_pairs={{0,2},{2,4},{4,6},{1,3},{3,5},{5,7},{8,10},{10,12},{12,14},{9,11},... | collective-permute-start | bytes 1572872 | tf_op jit(solution)/shard_map/ppermute | solution.py:15
  75.9 2.2 %copy-start.2 = (bf16[1024,2048]{1,0:T(8,128)(2,1)}, bf16[1024,2048]{1,0:T(8,128)(2,1)S(1)}, u32[]{:S(2)}) copy-start(bf16[1024,2048]{1,0:T(8,128)(2,1)S(1)} %fusion.17) | copy-start | bytes 12582916
  78.1 15.3 %collective-permute-start.3 = (bf16[128,2048]{1,0:T(8,128)(2,1)}, bf16[128,2048]{1,0:T(8,128)(2,1)S(1)}, u32[]{:S(2)}, u32[]{:S(2)}) collective-permute-start(bf16[128,2048]{1,0:T(8,128)(2,1)} %slice.15), channel_id=1, source_target_pairs={{0,2},{2,4},{4,6},{1,3},{3,5},{5,7},{8,10},{10,12},{12,14},{9,11},... | collective-permute-start | bytes 1572872 | tf_op jit(solution)/shard_map/ppermute | solution.py:15
  80.6 2.2 %copy-start.3 = (bf16[1024,2048]{1,0:T(8,128)(2,1)S(1)}, bf16[1024,2048]{1,0:T(8,128)(2,1)}, u32[]{:S(2)}) copy-start(bf16[1024,2048]{1,0:T(8,128)(2,1)} %copy-done.2) | copy-start | bytes 12582916
  84.2 3.2 %copy-start.1 = (bf16[1024,2048]{1,0:T(8,128)(2,1)S(1)}, bf16[1024,2048]{1,0:T(8,128)(2,1)}, u32[]{:S(2)}) copy-start(bf16[1024,2048]{1,0:T(8,128)(2,1)} %copy-done) | copy-start | bytes 12582916
  96.9 2.1 %copy-start.4 = (f32[9,16,64,128]{3,2,1,0:T(8,128)}, f32[9,16,64,128]{3,2,1,0:T(8,128)S(1)}, u32[]{:S(2)}) copy-start(f32[9,16,64,128]{3,2,1,0:T(8,128)S(1)} %fusion.1) | copy-start | bytes 14155780
